TPU v7x, 128 devices: a whole 4x4x4 slice. The times are simulated.
128 devices in a mesh: sta: 16 (over x, y_hi, core), freq: 8 (over y_lo, z).
Axes of the slice: x: 4, y: 4 (y_hi: 2, y_lo: 2; y = y_hi * 2 + y_lo), z: 4, core: 2. Of those that a mesh axis runs over, the one named last changes fastest.
Arguments:
- records: bfloat16 [2048, 256, 512], P('sta', 'freq'), may hold values from -6 to 6
- available: int32 [2048, 256], P('sta', 'freq'), may hold values 0 or 1
Outputs:
- cross_gram: bfloat16 [2, 128, 2048, 2048], P(None, 'freq', 'sta')
All inputs are finite; a program needn't handle non-finite values. No bound on the sum of `available` on one device may be relied on, other than what follows from the above.
Results may differ from a plain program's by a relative error of at most 0.0056.
Values may be sent and summed in bfloat16 or wider, within the bound.
No kernel may reach another device: no remote copies, remote signals or barrier semaphores. Data moves between devices by JAX's collectives and lax.ppermute only.
A program may use at most 192 MiB of HBM per device.

v0:
```python
import jax
import jax.numpy as jnp
from jax import lax
from jax.sharding import PartitionSpec as P

FFT_LEN = 512
BINS = 128
BAND_LO = 16


def spectra_table():
    sample_idx = jnp.arange(FFT_LEN, dtype=jnp.int32)[:, None]
    bin_idx = BAND_LO + jnp.arange(BINS, dtype=jnp.int32)[None, :]
    phase = (sample_idx * bin_idx % FFT_LEN).astype(jnp.float32) * (2.0 * jnp.pi / FFT_LEN)
    return jnp.concatenate([jnp.cos(phase), -jnp.sin(phase)], axis=1)


def gram_block(mine, other):
    count = mine.shape[3]
    both_real = jnp.einsum(
        "fas,fbs->fab", mine[:, 0], other[:, 0], preferred_element_type=jnp.float32
    )
    both_imag = jnp.einsum(
        "fas,fbs->fab", mine[:, 1], other[:, 1], preferred_element_type=jnp.float32
    )
    imag_real = jnp.einsum(
        "fas,fbs->fab", mine[:, 1], other[:, 0], preferred_element_type=jnp.float32
    )
    real_imag = jnp.einsum(
        "fas,fbs->fab", mine[:, 0], other[:, 1], preferred_element_type=jnp.float32
    )
    return jnp.stack([(both_real + both_imag) / count, (imag_real - real_imag) / count]).astype(
        jnp.bfloat16
    )


def shards(records, available):
    stations, segments, samples = records.shape
    sample_pos = jnp.arange(samples, dtype=jnp.float32)
    window_taper = 0.5 - 0.5 * jnp.cos(2.0 * jnp.pi * sample_pos / samples)
    tapered = records.astype(jnp.float32) * window_taper
    spectra = jnp.dot(
        tapered.reshape(stations * segments, samples),
        spectra_table(),
        precision=lax.Precision.HIGHEST,
        preferred_element_type=jnp.float32,
    )
    spectra = spectra.reshape(stations, segments, 2 * BINS)
    real_part = spectra[..., :BINS]
    imag_part = spectra[..., BINS:]
    power = jnp.mean(real_part * real_part + imag_part * imag_part, axis=-1, keepdims=True)
    weight = available.astype(jnp.float32)[..., None] / jnp.sqrt(power + 1e-05)
    whitened = jnp.stack([real_part * weight, imag_part * weight]).astype(jnp.bfloat16)
    whitened = jnp.transpose(whitened, (3, 0, 1, 2))
    panel = lax.all_to_all(whitened, "freq", split_axis=0, concat_axis=3, tiled=True)
    return gram_block(panel, lax.all_gather(panel, "sta", axis=2, tiled=True))


def solution(mesh):
    in_specs = (P("sta", "freq", None), P("sta", "freq"))
    out_specs = P(None, "freq", "sta", None)
    return jax.shard_map(shards, mesh=mesh, in_specs=in_specs, out_specs=out_specs, check_vma=False)
```

profile of v0, /device:TPU:1, one launch (start us, length us, event | category | flops | bytes accessed | tf_op | source)
XLA Modules:
  0.0 333.4 jit_solution(14007002556690948768)
XLA Ops:
  6.5 0.0 all-gather.2.cloned.1.call-start
  6.6 1.1 fusion.18
  7.6 3.4 %convert_multiply_fusion = f32[128,32,512]{2,1,0:T(8,128)S(1)} fusion(bf16[128,32,512]{2,1,0:T(8,128)(2,1)} %param.2, f32[512]{0:T(512)S(1)} %multiply_subtract_fusion), kind=kLoop, calls=%fused_computation.13 | loop fusion | flops 4194304 | bytes 12584960 | tf_op jit(solution)/shard_map/mul | solution.py:41
  11.1 0.0 copy-start.2
  11.1 11.3 %fusion.6 = f32[128,32,256]{2,0,1:T(8,128)S(1)} fusion(f32[128,32,512]{2,1,0:T(8,128)S(1)} %convert_multiply_fusion, f32[512,128]{1,0:T(8,128)S(1)} %get-tuple-element.8, f32[512,128]{1,0:T(8,128)S(1)} %get-tuple-element.7), kind=kOutput, calls=%fused_computation.11 | convolution fusion | flops 6442582016 | bytes 13107200 | tf_op jit(solution)/shard_map/dot_general | solution.py:42
  22.4 0.6 add_reduce_fusion
  23.0 0.0 copy-done.2
  23.0 0.8 fusion.8
  23.9 0.2 maximum_bitcast_fusion
  24.1 2.9 copy.12
  27.0 32.6 %all_to_all.18 = bf16[128,2,128,32]{2,3,1,0:T(8,128)(2,1)S(1)} all-to-all(bf16[128,2,128,32]{2,3,1,0:T(8,128)(2,1)} %copy.12), channel_id=1, replica_groups=mesh['sta'=16,'freq'=8] {'freq'}, dimensions={0} | all-to-all | bytes 4194304 | tf_op jit(solution)/shard_map/all_to_all | solution.py:55
  59.5 0.5 copy.13
  60.0 2.6 copy.14
  62.6 0.0 all-gather.2.cloned.1.call-update
  62.6 0.0 copy-start.1
  62.7 188.9 %all-gather.2.cloned.1.call-done = bf16[16,2,2048,256]{3,2,0,1:T(8,128)(2,1)} async-done(((bf16[16,2,128,256]{3,2,0,1:T(8,128)(2,1)}), bf16[16,2,2048,256]{3,2,0,1:T(8,128)(2,1)}) %all-gather.2.cloned.1.call-update) | async-done | bytes 33554448 | tf_op jit(solution)/shard_map/all_gather | solution.py:56
  251.6 12.8 %fusion = f32[16,128,2048]{2,1,0:T(8,128)} fusion(bf16[16,2,2048,256]{3,2,0,1:T(8,128)(2,1)} %all-gather.2.cloned.1.call-done, bf16[16,2,128,256]{3,2,0,1:T(8,128)(2,1)} %copy.14), kind=kOutput, calls=%fused_computation.5 | convolution fusion | flops 2147483648 | bytes 34603008 | tf_op jit(solution)/shard_map/fas,fbs->fab/dot_general | solution.py:26
  264.4 0.0 copy-done.1
  264.4 12.3 %fusion.1 = f32[16,128,2048]{2,1,0:T(8,128)} fusion(bf16[16,2,2048,256]{3,2,0,1:T(8,128)(2,1)} %all-gather.2.cloned.1.call-done, bf16[16,2,128,256]{3,2,0,1:T(8,128)(2,1)S(1)} %copy-done.1), kind=kOutput, calls=%fused_computation.6 | convolution fusion | flops 2147483648 | bytes 34603008 | tf_op jit(solution)/shard_map/fas,fbs->fab/dot_general | solution.py:20
  276.6 0.0 copy-start
  276.6 15.5 %fusion.5 = bf16[1,16,128,2048]{3,2,1,0:T(8,128)(2,1)} fusion(f32[16,128,2048]{2,1,0:T(8,128)} %fusion, bf16[16,2,2048,256]{3,2,0,1:T(8,128)(2,1)} %all-gather.2.cloned.1.call-done, bf16[16,2,128,256]{3,2,0,1:T(8,128)(2,1)S(1)} %copy-done.1), kind=kOutput, calls=%fused_computation.10 | convolution fusion | flops 2160066560 | bytes 42991616 | tf_op jit(solution)/shard_map/fas,fbs->fab/dot_general | solution.py:29
  292.1 2.9 copy-done
  295.1 17.7 %fusion.4 = bf16[1,16,128,2048]{3,2,1,0:T(8,128)(2,1)} fusion(f32[16,128,2048]{2,1,0:T(8,128)S(1)} %copy-done, bf16[16,2,2048,256]{3,2,0,1:T(8,128)(2,1)} %all-gather.2.cloned.1.call-done, bf16[16,2,128,256]{3,2,0,1:T(8,128)(2,1)S(1)} %copy-done.1), kind=kOutput, calls=%fused_computation.9 | convolution fusion | flops 2160066560 | bytes 42991616 | tf_op jit(solution)/shard_map/fas,fbs->fab/dot_general | solution.py:23
  312.8 13.8 %pad_maximum_fusion = bf16[2,16,128,2048]{3,2,1,0:T(8,128)(2,1)} fusion(bf16[1,16,128,2048]{3,2,1,0:T(8,128)(2,1)} %fusion.5, bf16[1,16,128,2048]{3,2,1,0:T(8,128)(2,1)} %fusion.4), kind=kLoop, calls=%fused_computation.2 | loop fusion | flops 8388608 | bytes 33554432 | tf_op jit(solution)/shard_map/stack | solution.py:32
  (3 shorter events, 0.1 us)
Async XLA Ops:
  6.5 245.0 %all-gather.2.cloned.1.call-start = ((), (), s32[]{:S(2)}) async-start(), calls=%async_computation.1 | async-start | bytes 35651584 | tf_op jit(solution)/shard_map/all_gather | solution.py:56
  11.1 11.9 %copy-start.2 = (s32[128,32]{0,1:T(8,128)S(1)}, s32[128,32]{0,1:T(8,128)}, u32[]{:S(2)}) copy-start(s32[128,32]{0,1:T(8,128)} %param.3) | copy-start | bytes 49156
  62.6 201.7 %copy-start.1 = (bf16[16,2,128,256]{3,2,0,1:T(8,128)(2,1)S(1)}, bf16[16,2,128,256]{3,2,0,1:T(8,128)(2,1)}, u32[]{:S(2)}) copy-start(bf16[16,2,128,256]{3,2,0,1:T(8,128)(2,1)} %copy.14) | copy-start | bytes 6291460
  276.6 18.4 %copy-start = (f32[16,128,2048]{2,1,0:T(8,128)S(1)}, f32[16,128,2048]{2,1,0:T(8,128)}, u32[]{:S(2)}) copy-start(f32[16,128,2048]{2,1,0:T(8,128)} %fusion.1) | copy-start | bytes 50331652
Sparse Core Ops, SparseCore 0:
  62.8 188.7 all-gather.1
where the time goes:
time: 334 us; the launch traced here: 333 us
  waiting for transfers between devices  189 us (57%)
  matrix products  69.5 us (21%)
  blocking collectives  32.6 us (10%)
  other arithmetic  20 us (6%)
  between operations  13.5 us (4%)
  local copies, waits for them, and re-layouts  8.93 us (3%)
    all_gather x1, waiting for transfers between devices, shards(): return gram_block(panel, lax.all_gather(panel, 'sta', axis=2, tiled=True))  189 us
    all_to_all x1, blocking collectives, shards(): lax.all_to_all(whitened, 'freq', split_axis=0, concat_axis=3, tiled=True)  32.6 us
    dot_general x1, matrix products, gram_block(): jnp.einsum('fas,fbs->fab', mine[:, 1], other[:, 1], preferred_element_typ...  17.7 us
    dot_general x1, matrix products, gram_block(): jnp.einsum('fas,fbs->fab', mine[:, 0], other[:, 1], preferred_element_typ...  15.5 us
    another operation x1, other arithmetic, gram_block(): jnp.stack([(both_real + both_imag) / count, (imag_real - real_imag) / cou...  13.8 us
    dot_general x1, matrix products, gram_block(): jnp.einsum('fas,fbs->fab', mine[:, 1], other[:, 0], preferred_element_typ...  12.8 us
    dot_general x1, matrix products, gram_block(): jnp.einsum('fas,fbs->fab', mine[:, 0], other[:, 0], preferred_element_typ...  12.3 us
    dot_general x1, matrix products, shards(): jnp.dot(tapered.reshape(stations * segments, samples), spectra_table(), p...  11.3 us
  transfers between devices with their start and end apart: 1, of which 1 were waited for; matrix products, arithmetic and copies ran while one was open for 0% of the time, Pallas kernels for 0%

commit v1 on v0

--- a/solution.py
+++ b/solution.py
@@ -53,7 +53,12 @@
     whitened = jnp.stack([real_part * weight, imag_part * weight]).astype(jnp.bfloat16)
     whitened = jnp.transpose(whitened, (3, 0, 1, 2))
     panel = lax.all_to_all(whitened, "freq", split_axis=0, concat_axis=3, tiled=True)
-    return gram_block(panel, lax.all_gather(panel, "sta", axis=2, tiled=True))
+    return gram_block(
+        panel,
+        jnp.concatenate(
+            lax.all_to_all(jnp.stack([panel] * lax.axis_size("sta")), "sta", 0, 0), axis=2
+        ),
+    )
 
 
 def solution(mesh):

time: 334 us -> 542 us (1.62)
  blocking collectives: 32.6 us -> 408 us
  waiting for transfers between devices: 189 us -> 0 us
  local copies, waits for them, and re-layouts: 8.93 us -> 44.3 us
  between operations: 13.5 us -> 0.08 us
    all_to_all x0 -> x1, blocking collectives: none -> 375 us  [shards(): lax.all_to_all(jnp.stack([panel] * lax.axis_size('sta')), 'sta', 0, 0)]
    all_gather x1 -> x0, waiting for transfers between devices: 189 us -> none  [shards(): return gram_block(panel, lax.all_gather(panel, 'sta', axis=2, tiled=True))]
    reshape x0 -> x1, local copies, waits for them, and re-layouts: none -> 22.7 us  [shards(): jnp.concatenate(lax.all_to_all(jnp.stack([panel] * lax.axis_size('sta')),...]
    another operation x0 -> x1, local copies, waits for them, and re-layouts: none -> 11.1 us  [shards(): jnp.stack([panel] * lax.axis_size('sta'))]
  transfers between devices with their start and end apart: 1 -> 0, of which waited for: 1 -> 0; matrix products, arithmetic and copies ran while one was open for 0% -> 0% of each run, Pallas kernels for 0% -> 0%
where the time goes in v1:
time: 542 us; the launch traced here: 541 us
  blocking collectives  408 us (75%)
  matrix products  69.1 us (13%)
  local copies, waits for them, and re-layouts  44.3 us (8%)
  other arithmetic  20 us (4%)
    all_to_all x1, blocking collectives, shards(): lax.all_to_all(jnp.stack([panel] * lax.axis_size('sta')), 'sta', 0, 0)  375 us
    all_to_all x1, blocking collectives, shards(): lax.all_to_all(whitened, 'freq', split_axis=0, concat_axis=3, tiled=True)  32.6 us
    reshape x1, local copies, waits for them, and re-layouts, shards(): jnp.concatenate(lax.all_to_all(jnp.stack([panel] * lax.axis_size('sta')),...  22.7 us
    dot_general x1, matrix products, gram_block(): jnp.einsum('fas,fbs->fab', mine[:, 1], other[:, 1], preferred_element_typ...  17.6 us
    dot_general x1, matrix products, gram_block(): jnp.einsum('fas,fbs->fab', mine[:, 0], other[:, 1], preferred_element_typ...  15.5 us
    another operation x1, other arithmetic, gram_block(): jnp.stack([(both_real + both_imag) / count, (imag_real - real_imag) / cou...  13.8 us
    dot_general x1, matrix products, gram_block(): jnp.einsum('fas,fbs->fab', mine[:, 1], other[:, 0], preferred_element_typ...  12.5 us
    dot_general x1, matrix products, gram_block(): jnp.einsum('fas,fbs->fab', mine[:, 0], other[:, 0], preferred_element_typ...  12.3 us

profile of v1, /device:TPU:1, one launch (start us, length us, event | category | flops | bytes accessed | tf_op | source)
XLA Modules:
  0.0 541.1 jit_solution(5550109565792005117)
XLA Ops:
  0.1 1.1 fusion.18
  1.1 3.4 convert_multiply_fusion
  4.5 0.0 copy-start.1
  4.6 11.3 %fusion.6 = f32[128,32,256]{2,0,1:T(8,128)S(1)} fusion(f32[128,32,512]{2,1,0:T(8,128)S(1)} %convert_multiply_fusion, f32[512,128]{1,0:T(8,128)S(1)} %get-tuple-element.8, f32[512,128]{1,0:T(8,128)S(1)} %get-tuple-element.7), kind=kOutput, calls=%fused_computation.11 | convolution fusion | flops 6442582016 | bytes 13107200 | tf_op jit(solution)/shard_map/dot_general | solution.py:42
  15.9 0.6 add_reduce_fusion
  16.5 0.0 copy-done.1
  16.5 0.8 fusion.8
  17.3 0.2 maximum_bitcast_fusion
  17.5 2.9 copy.12
  20.4 32.6 %all_to_all.23 = bf16[128,2,128,32]{2,3,1,0:T(8,128)(2,1)S(1)} all-to-all(bf16[128,2,128,32]{2,3,1,0:T(8,128)(2,1)} %copy.12), channel_id=1, replica_groups=mesh['sta'=16,'freq'=8] {'freq'}, dimensions={0} | all-to-all | bytes 4194304 | tf_op jit(solution)/shard_map/all_to_all | solution.py:55
  53.0 1.8 copy.13
  54.8 2.9 copy.14
  57.7 11.1 %stack.46 = bf16[16,16,2,128,256]{4,3,1,2,0:T(8,128)(2,1)} broadcast(bf16[16,2,128,256]{3,2,0,1:T(8,128)(2,1)S(1)} %copy.14), dimensions={1,2,3,4} | broadcast | bytes 35651584 | tf_op jit(solution)/shard_map/stack | solution.py:59
  68.7 375.1 %all_to_all.24 = bf16[16,16,2,128,256]{4,3,1,2,0:T(8,128)(2,1)} all-to-all(bf16[16,16,2,128,256]{4,3,1,2,0:T(8,128)(2,1)} %stack.46), channel_id=1, replica_groups=mesh['sta'=16,'freq'=8] {'sta'}, dimensions={0} | all-to-all | bytes 67108864 | tf_op jit(solution)/shard_map/all_to_all | solution.py:59
  443.8 22.7 %copy.16 = bf16[16,2,16,128,256]{4,3,2,0,1:T(8,128)(2,1)} copy(bf16[16,2,16,128,256]{4,3,0,1,2:T(8,128)(2,1)} %bitcast.43) | data formatting | bytes 67108864 | tf_op jit(solution)/shard_map/reshape | solution.py:58
  466.5 12.5 %fusion = f32[16,128,2048]{2,1,0:T(8,128)} fusion(bf16[16,2,2048,256]{3,2,0,1:T(8,128)(2,1)} %bitcast.39, bf16[16,2,128,256]{3,2,0,1:T(8,128)(2,1)S(1)} %copy.14), kind=kOutput, calls=%fused_computation.5 | convolution fusion | flops 2147483648 | bytes 34603008 | tf_op jit(solution)/shard_map/fas,fbs->fab/dot_general | solution.py:26
  479.0 12.3 %fusion.1 = f32[16,128,2048]{2,1,0:T(8,128)} fusion(bf16[16,2,2048,256]{3,2,0,1:T(8,128)(2,1)} %bitcast.40, bf16[16,2,128,256]{3,2,0,1:T(8,128)(2,1)S(1)} %copy.14), kind=kOutput, calls=%fused_computation.6 | convolution fusion | flops 2147483648 | bytes 34603008 | tf_op jit(solution)/shard_map/fas,fbs->fab/dot_general | solution.py:20
  491.3 0.0 copy-start
  491.3 15.5 %fusion.5 = bf16[1,16,128,2048]{3,2,1,0:T(8,128)(2,1)} fusion(f32[16,128,2048]{2,1,0:T(8,128)} %fusion, bf16[16,2,2048,256]{3,2,0,1:T(8,128)(2,1)} %bitcast.41, bf16[16,2,128,256]{3,2,0,1:T(8,128)(2,1)S(1)} %copy.14), kind=kOutput, calls=%fused_computation.10 | convolution fusion | flops 2160066560 | bytes 42991616 | tf_op jit(solution)/shard_map/fas,fbs->fab/dot_general | solution.py:29
  506.7 2.9 copy-done
  509.7 17.6 %fusion.4 = bf16[1,16,128,2048]{3,2,1,0:T(8,128)(2,1)} fusion(f32[16,128,2048]{2,1,0:T(8,128)S(1)} %copy-done, bf16[16,2,2048,256]{3,2,0,1:T(8,128)(2,1)} %bitcast.42, bf16[16,2,128,256]{3,2,0,1:T(8,128)(2,1)S(1)} %copy.14), kind=kOutput, calls=%fused_computation.9 | convolution fusion | flops 2160066560 | bytes 42991616 | tf_op jit(solution)/shard_map/fas,fbs->fab/dot_general | solution.py:23
  527.3 13.8 %pad_maximum_fusion = bf16[2,16,128,2048]{3,2,1,0:T(8,128)(2,1)} fusion(bf16[1,16,128,2048]{3,2,1,0:T(8,128)(2,1)} %fusion.5, bf16[1,16,128,2048]{3,2,1,0:T(8,128)(2,1)} %fusion.4), kind=kLoop, calls=%fused_computation.2 | loop fusion | flops 8388608 | bytes 33554432 | tf_op jit(solution)/shard_map/stack | solution.py:32
  (3 shorter events, 0.1 us)
Async XLA Ops:
  4.5 11.9 %copy-start.1 = (s32[128,32]{0,1:T(8,128)S(1)}, s32[128,32]{0,1:T(8,128)}, u32[]{:S(2)}) copy-start(s32[128,32]{0,1:T(8,128)} %param.3) | copy-start | bytes 49156
  491.3 18.4 %copy-start = (f32[16,128,2048]{2,1,0:T(8,128)S(1)}, f32[16,128,2048]{2,1,0:T(8,128)}, u32[]{:S(2)}) copy-start(f32[16,128,2048]{2,1,0:T(8,128)} %fusion.1) | copy-start | bytes 50331652
